TPU v7x, 256 devices: a whole 4x4x8 slice. The times are simulated.
256 devices in a mesh: dp: 64 (over z, y, x_hi), mp: 4 (over x_lo, core).
Axes of the slice: x: 4 (x_hi: 2, x_lo: 2; x = x_hi * 2 + x_lo), y: 4, z: 8, core: 2. Of those that a mesh axis runs over, the one named last changes fastest.
Arguments:
- hidden_states: bfloat16 [32768, 3584], P('dp'), may hold values from -6 to 6
- token_ids: int32 [2048, 16], P('dp'), may hold values from 0 to 152063, as said below
- norm_gain: float32 [3584], replicated, may hold values from 0.5 to 1.5
- q_weight: bfloat16 [3584, 3584], P('dp', 'mp'), may hold values from -0.09375 to 0.09375
- key_matrix: bfloat16 [3584, 512], P('dp', 'mp'), may hold values from -0.09375 to 0.09375
- value_matrix: bfloat16 [3584, 512], P('dp', 'mp'), may hold values from -0.09375 to 0.09375
- out_weight: bfloat16 [3584, 3584], P('dp', 'mp'), may hold values from -0.09375 to 0.09375
- label_table: bfloat16 [65536, 3584], P(('dp', 'mp')), may hold values from -6 to 6
- refresh_rows: int32 [2048], P(('dp', 'mp')), may hold values from 0 to 255, as said below
- label_counts: int32 [65536], P(('dp', 'mp')), may hold values from 1 to 8191
- queries: bfloat16 [128, 3584], replicated, may hold values from -6 to 6
- positives: int32 [128, 8], replicated, may hold values from 0 to 65535
Outputs:
- label_grad: float32 [65536, 3584], P(('dp', 'mp'))
- query_grad: float32 [128, 3584], replicated
- loss: float32 [], replicated
Inputs may be any that keep to these rules, and one draw needn't show every extreme that they name: `token_ids`: in every text the first id is not 0, and after an id 0 all later ids of that text are 0. `refresh_rows`: the 8 entries of each aligned block of 8 entries are distinct.
All inputs are finite; a program needn't handle non-finite values.
Results may differ from a plain program's by a relative error of at most 0.003.
Values may be sent and summed in bfloat16 or wider, within the bound.
No kernel may reach another device: no remote copies, remote signals or barrier semaphores. Data moves between devices by JAX's collectives and lax.ppermute only.
A program may use at most 128 MiB of HBM per device.

v0:
```python
import math
import jax
import jax.numpy as jnp
from jax import lax
from jax.sharding import PartitionSpec as P

HEAD_WIDTH = 128
rope_theta = 1000000.0
norm_eps = 1e-06
focal_beta = 0.9999


def rotary(values, head_size):
    length = values.shape[1]
    half = head_size // 2
    frequency = rope_theta ** (-2.0 * jnp.arange(half, dtype=jnp.float32) / head_size)
    angles = jnp.arange(length, dtype=jnp.float32)[:, None] * frequency[None, :]
    cosine = jnp.concatenate([jnp.cos(angles), jnp.cos(angles)], axis=1)[None, :, None, :]
    sine = jnp.concatenate([jnp.sin(angles), jnp.sin(angles)], axis=1)[None, :, None, :]
    turned = jnp.concatenate([-values[..., half:], values[..., :half]], axis=-1)
    return values * cosine + turned * sine


def attend(query_rows, key_rows, value_rows, text_ids, head_size):
    texts, length = text_ids.shape
    kv_heads = key_rows.shape[1] // head_size
    repeat = query_rows.shape[1] // head_size // kv_heads
    query_r = query_rows.reshape(texts, length, kv_heads, repeat, head_size)
    key_r = key_rows.reshape(texts, length, kv_heads, head_size)
    value_r = value_rows.reshape(texts, length, kv_heads, head_size)
    scores = jnp.einsum(
        "ntgrd,nsgd->ngrts", query_r, key_r, preferred_element_type=jnp.float32
    ) / math.sqrt(head_size)
    causal = jnp.arange(length)[:, None] >= jnp.arange(length)[None, :]
    allowed = causal[None, None, None, :, :] & (text_ids != 0)[:, None, None, None, :]
    weights = jnp.where(allowed, jnp.exp(scores), 0.0)
    probs = (weights / jnp.sum(weights, axis=-1, keepdims=True)).astype(jnp.bfloat16)
    mixed = jnp.einsum("ngrts,nsgd->ntgrd", probs, value_r, preferred_element_type=jnp.float32)
    return mixed.reshape(texts * length, -1).astype(jnp.bfloat16)


def shards(
    hidden_states,
    token_ids,
    norm_gain,
    q_weight,
    key_matrix,
    value_matrix,
    out_weight,
    label_table,
    refresh_rows,
    label_counts,
    queries,
    positives,
):
    width = hidden_states.shape[1]
    group_tokens = hidden_states.shape[0]
    texts, length = token_ids.shape
    states = hidden_states.astype(jnp.float32)
    scaled = lax.rsqrt(jnp.mean(states * states, axis=1, keepdims=True) + norm_eps)
    normed = (states * scaled * norm_gain).astype(jnp.bfloat16)
    pieces = (
        lax.all_gather(q_weight, "dp", axis=0, tiled=True),
        lax.all_gather(key_matrix, "dp", axis=0, tiled=True),
        lax.all_gather(value_matrix, "dp", axis=0, tiled=True),
    )
    query_raw, key_raw, value_raw = tuple(
        (jnp.dot(normed, piece, preferred_element_type=jnp.float32) for piece in pieces)
    )
    queries_rot = (
        rotary(query_raw.reshape(texts, length, -1, HEAD_WIDTH), HEAD_WIDTH)
        .reshape(group_tokens, -1)
        .astype(jnp.bfloat16)
    )
    rotary_keys = (
        rotary(key_raw.reshape(texts, length, -1, HEAD_WIDTH), HEAD_WIDTH)
        .reshape(group_tokens, -1)
        .astype(jnp.bfloat16)
    )
    values_rot = value_raw.astype(jnp.bfloat16)
    attended = attend(queries_rot, rotary_keys, values_rot, token_ids, HEAD_WIDTH)
    live = (token_ids != 0).astype(jnp.float32)
    share = texts // lax.axis_size("mp")
    member = lax.axis_index("mp")
    live_own = lax.dynamic_slice_in_dim(live, member * share, share, 0)
    states_own = lax.dynamic_slice_in_dim(
        states, member * share * length, share * length, 0
    ).reshape(share, length, width)
    counted = jnp.sum(live_own, axis=1, keepdims=True)
    head_terms = lax.dot_general(
        attended,
        lax.all_gather(out_weight, "dp", axis=0, tiled=True),
        (((1,), (1,)), ((), ())),
        preferred_element_type=jnp.float32,
    )
    output_own = lax.psum_scatter(head_terms, "mp", scatter_dimension=0, tiled=True).reshape(
        share, length, width
    )
    refreshed = (
        jnp.sum((states_own + output_own) * live_own[:, :, None], axis=1) / counted
    ).astype(jnp.bfloat16)
    table = label_table.at[refresh_rows].set(refreshed)
    root = math.sqrt(width)
    owned = label_table.shape[0]
    logits = (
        lax.dot_general(
            queries, table, (((1,), (1,)), ((), ())), preferred_element_type=jnp.float32
        )
        / root
    )
    first_label = (lax.axis_index("dp") * lax.axis_size("mp") + member) * owned
    label_ids = first_label + jnp.arange(owned, dtype=jnp.int32)
    matched = jnp.any(positives[:, :, None] == label_ids[None, None, :], axis=1)
    signs = jnp.where(matched, 1.0, -1.0)
    margin = signs * logits
    balance = (1.0 - focal_beta) / -jnp.expm1(
        label_counts.astype(jnp.float32) * math.log(focal_beta)
    )
    missed = jax.nn.sigmoid(-margin)
    softened = jax.nn.softplus(-margin)
    focal_terms = balance[None, :] * missed * missed * softened
    slopes = (
        balance[None, :]
        * signs
        * (-(missed * missed) * (2.0 * jax.nn.sigmoid(margin) * softened + missed))
    ).astype(jnp.bfloat16)
    query_part = jnp.dot(slopes, table, preferred_element_type=jnp.float32) / root
    label_part = (
        lax.dot_general(
            slopes, queries, (((0,), (0,)), ((), ())), preferred_element_type=jnp.float32
        )
        / root
    )
    query_sum, loss_sum, summed_weight = lax.psum(
        (query_part, jnp.sum(focal_terms), jnp.sum(balance)), ("dp", "mp")
    )
    total_labels = owned * lax.axis_size("dp") * lax.axis_size("mp")
    factor = total_labels / summed_weight
    loss = factor * loss_sum / (queries.shape[0] * total_labels)
    return (factor * label_part, factor * query_sum, loss)


def solution(mesh):
    in_specs = (
        P("dp", None),
        P("dp", None),
        P(),
        P("dp", "mp"),
        P("dp", "mp"),
        P("dp", "mp"),
        P("dp", "mp"),
        P(("dp", "mp"), None),
        P(("dp", "mp")),
        P(("dp", "mp")),
        P(),
        P(),
    )
    out_specs = (P(("dp", "mp"), None), P(), P())
    return jax.shard_map(shards, mesh=mesh, in_specs=in_specs, out_specs=out_specs, check_vma=False)
```

profile of v0, /device:TPU:2, one launch (start us, length us, event | category | flops | bytes accessed | tf_op | source)
XLA Modules:
  0.0 762.3 jit_solution(14979798838357729430)
XLA Ops:
  7.2 0.7 all-gather.3.cloned.1.call-update
  8.0 0.7 all-gather.5.cloned.1.call-update
  9.0 3.0 multiply_reduce_fusion
  12.0 190.2 %all_gather.13 = bf16[3584,128]{1,0:T(8,128)(2,1)S(1)} all-gather(bf16[56,128]{1,0:T(8,128)(2,1)S(1)} %copy-done.4), channel_id=1, replica_groups=mesh['dp'=64,'mp'=4] {'dp'}, dimensions={0}, use_global_device_ids=true | all-gather | bytes 931840 | tf_op jit(solution)/shard_map/all_gather | solution.py:64
  202.2 1.2 fusion.23
  203.8 180.0 %all_gather.12 = bf16[3584,128]{1,0:T(8,128)(2,1)S(1)} all-gather(bf16[56,128]{1,0:T(8,128)(2,1)S(1)} %copy-done.5), channel_id=1, replica_groups=mesh['dp'=64,'mp'=4] {'dp'}, dimensions={0}, use_global_device_ids=true | all-gather | bytes 931840 | tf_op jit(solution)/shard_map/all_gather | solution.py:65
  383.8 1.2 convolution_convert_fusion.1
  385.0 9.2 %fusion.22 = f32[512,896]{1,0:T(8,128)} fusion(bf16[3584,896]{1,0:T(8,128)(2,1)} %all-gather.3.cloned.1.call-done, f32[3584]{0:T(1024)S(1)} %copy-done.9, f32[512]{0:T(512)S(1)} %add_rsqrt_fusion, bf16[512,3584]{1,0:T(8,128)(2,1)} %param.12), kind=kOutput, calls=%fused_computation.58 | convolution fusion | flops 3295674368 | bytes 11943936 | tf_op jit(solution)/shard_map/dot_general | solution.py:68
  394.2 1.6 reshape.123
  395.8 0.8 slice_negate_fusion
  396.5 0.6 maximum_multiply_fusion
  397.2 0.2 mul.215
  397.4 1.3 copy-done.3
  398.7 1.0 fusion
  399.7 1.0 reshape.124
  400.7 2.0 fusion.25
  402.8 0.5 fusion.1
  403.2 0.3 copy.31
  403.6 8.9 %fusion.4 = f32[512,3584]{1,0:T(8,128)} fusion(bf16[3584,896]{1,0:T(8,128)(2,1)} %all-gather.5.cloned.1.call-done, bf16[64,8,7,128]{3,2,1,0:T(8,128)(2,1)S(1)} %bitcast.69), kind=kOutput, calls=%fused_computation.21 | convolution fusion | flops 3288334336 | bytes 14680064 | tf_op jit(solution)/shard_map/dot_general | solution.py:90
  412.5 0.3 all-reduce.3.cloned.1.call-start
  412.8 6.0 convert_element_type.43
  419.1 0.4 compare_reduce_fusion
  419.7 0.6 fusion.24
  420.3 60.5 %reduce-scatter.2.cloned.1.call-done = f32[128,3584]{1,0:T(8,128)} async-done(((f32[512,3584]{1,0:T(8,128)}), f32[128,3584]{1,0:T(8,128)}) %reduce-scatter.2.cloned.1.call-update) | async-done | bytes 1835024 | tf_op jit(solution)/shard_map/reduce_scatter | solution.py:96
  480.9 2.5 multiply_reduce_fusion.1
  483.4 1.8 scatter_custom_fusion
  485.3 1.3 fusion.14
  486.6 1.8 convolution_multiply_fusion.1
  488.4 78.1 %all-reduce = (f32[]{:T(128)}, f32[]{:T(128)}) all-reduce(f32[]{:T(128)} %get-tuple-element.5, f32[]{:T(128)} %get-tuple-element.15), channel_id=1, replica_groups=mesh['dp'=64,'mp'=4] {'dp','mp'}, use_global_device_ids=true, to_apply=%region_8.9 | all-reduce | flops 2 | bytes 16 | tf_op jit(solution)/shard_map/psum | solution.py:134
  567.8 2.6 convolution_multiply_fusion
  570.4 181.4 %all-reduce.3.cloned.1.call-done = f32[128,3584]{1,0:T(8,128)} async-done(((f32[128,3584]{1,0:T(8,128)}), f32[128,3584]{1,0:T(8,128)}) %all-reduce.3.cloned.1.call-update) | async-done | bytes 1835024 | tf_op jit(solution)/shard_map/psum | solution.py:134
  751.8 2.9 broadcast_multiply_fusion
  (45 shorter events, 1.4 us)
Async XLA Ops:
  7.2 478.1 %copy-start = (bf16[128,3584]{1,0:T(8,128)(2,1)S(1)}, bf16[128,3584]{1,0:T(8,128)(2,1)}, u32[]{:S(2)}) copy-start(bf16[128,3584]{1,0:T(8,128)(2,1)} %param.22) | copy-start | bytes 2752516
  7.2 1.5 copy-start.6
  7.2 377.8 %all-gather.3.cloned.1.call-start = ((), (), s32[]{:S(2)}) async-start(), calls=%async_computation.1 | async-start | bytes 6522880 | tf_op jit(solution)/shard_map/all_gather | solution.py:63
  7.2 4.8 copy-start.4
  7.9 395.6 %all-gather.5.cloned.1.call-start = ((), (), s32[]{:S(2)}) async-start(), calls=%async_computation.2 | async-start | bytes 6522880 | tf_op jit(solution)/shard_map/all_gather | solution.py:92
  8.7 472.2 %reduce-scatter.2.cloned.1.call-start = ((), (), s32[]{:S(2)}) async-start(), calls=%async_computation.3 | async-start | bytes 9175040 | tf_op jit(solution)/shard_map/reduce_scatter | solution.py:96
  9.0 193.2 %copy-start.1 = (bf16[512,3584]{1,0:T(8,128)(2,1)S(1)}, bf16[512,3584]{1,0:T(8,128)(2,1)}, u32[]{:S(2)}) copy-start(bf16[512,3584]{1,0:T(8,128)(2,1)} %param.12) | copy-start | bytes 11010052
  9.0 193.2 %copy-start.9 = (f32[3584]{0:T(1024)S(1)}, f32[3584]{0:T(1024)}, u32[]{:S(2)}) copy-start(f32[3584]{0:T(1024)} %param.14) | copy-start | bytes 43012
  202.2 1.6 copy-start.5
  397.2 1.5 copy-start.3
  412.5 339.3 %all-reduce.3.cloned.1.call-start = ((), (), s32[]{:S(2)}) async-start(), calls=%async_computation.4 | async-start | bytes 3670016 | tf_op jit(solution)/shard_map/psum | solution.py:134
  412.7 6.2 copy-start.7
  412.8 6.9 copy-start.10
  412.8 6.9 copy-start.8
  418.8 64.6 %copy-start.2 = (bf16[256,3584]{1,0:T(8,128)(2,1)S(1)}, bf16[256,3584]{1,0:T(8,128)(2,1)}, u32[]{:S(2)}) copy-start(bf16[256,3584]{1,0:T(8,128)(2,1)} %param.19) | copy-start | bytes 5505028
Sparse Core Ops, SparseCore 0:
  11.7 146.0 all-gather.2
  161.5 139.9 all-gather.4
  412.6 68.2 reduce-scatter.1
  488.6 263.1 all-reduce.2
where the time goes:
time: 763 us; the launch traced here: 762 us
  blocking collectives  448 us (59%)
  waiting for transfers between devices  243 us (32%)
  matrix products  28.6 us (4%)
  other arithmetic  20.5 us (3%)
  between operations  16.5 us (2%)
    all_gather x1, blocking collectives, shards(): lax.all_gather(key_matrix, 'dp', axis=0, tiled=True)  190 us
    psum x1, waiting for transfers between devices, shards(): lax.psum((query_part, jnp.sum(focal_terms), jnp.sum(balance)), ('dp', 'mp'))  181 us
    all_gather x1, blocking collectives, shards(): lax.all_gather(value_matrix, 'dp', axis=0, tiled=True)  180 us
    psum x1, blocking collectives, shards(): lax.psum((query_part, jnp.sum(focal_terms), jnp.sum(balance)), ('dp', 'mp'))  78.1 us
    reduce_scatter x1, waiting for transfers between devices, shards(): lax.psum_scatter(head_terms, 'mp', scatter_dimension=0, tiled=True)  60.5 us
  transfers between devices with their start and end apart: 4, of which 2 were waited for; matrix products, arithmetic and copies ran while one was open for 4% of the time, Pallas kernels for 0%

commit v1 on v0

--- a/solution.py
+++ b/solution.py
@@ -132,7 +132,7 @@
         / root
     )
     query_sum, loss_sum, summed_weight = lax.psum(
-        (query_part, jnp.sum(focal_terms), jnp.sum(balance)), ("dp", "mp")
+        lax.psum((query_part, jnp.sum(focal_terms), jnp.sum(balance)), "mp"), "dp"
     )
     total_labels = owned * lax.axis_size("dp") * lax.axis_size("mp")
     factor = total_labels / summed_weight

time: 763 us -> 1250 us (1.64)
  waiting for transfers between devices: 243 us -> 618 us
  blocking collectives: 448 us -> 562 us
    psum x1 -> x2, waiting for transfers between devices: 181 us -> 556 us  [the longest x1 497 us: shards(): lax.psum(lax.psum((query_part, jnp.sum(focal_terms), jnp.sum(balance)), '...]
    psum x1 -> x2, blocking collectives: 78.1 us -> 192 us  [the longest x1 184 us: shards(): lax.psum(lax.psum((query_part, jnp.sum(focal_terms), jnp.sum(balance)), '...]
  transfers between devices with their start and end apart: 4 -> 5, of which waited for: 2 -> 3; matrix products, arithmetic and copies ran while one was open for 4% -> 3% of each run, Pallas kernels for 0% -> 0%
where the time goes in v1:
time: 1250 us
  waiting for transfers between devices  618 us (49%)
  blocking collectives  562 us (45%)
  matrix products  28.6 us (2%)
  other arithmetic  20.5 us (2%)
  between operations  16.5 us (1%)
    psum x1, waiting for transfers between devices, shards(): lax.psum(lax.psum((query_part, jnp.sum(focal_terms), jnp.sum(balance)), '...  497 us
    all_gather x1, blocking collectives, shards(): lax.all_gather(key_matrix, 'dp', axis=0, tiled=True)  190 us
    psum x1, blocking collectives, shards(): lax.psum(lax.psum((query_part, jnp.sum(focal_terms), jnp.sum(balance)), '...  184 us
    all_gather x1, blocking collectives, shards(): lax.all_gather(value_matrix, 'dp', axis=0, tiled=True)  180 us
    reduce_scatter x1, waiting for transfers between devices, shards(): lax.psum_scatter(head_terms, 'mp', scatter_dimension=0, tiled=True)  60.5 us
    psum x1, waiting for transfers between devices, shards(): lax.psum((query_part, jnp.sum(focal_terms), jnp.sum(balance)), 'mp')  59.8 us
  transfers between devices with their start and end apart: 5, of which 3 were waited for; matrix products, arithmetic and copies ran while one was open for 3% of the time, Pallas kernels for 0%

profile of v1, /device:TPU:2, one launch (start us, length us, event | category | flops | bytes accessed | tf_op | source)
XLA Modules:
  0.0 1251.5 jit_solution(4005259516998585319)
XLA Ops:
  7.2 0.7 all-gather.3.cloned.1.call-update
  8.0 0.7 all-gather.5.cloned.1.call-update
  9.0 3.0 multiply_reduce_fusion
  12.0 190.2 %all_gather.13 = bf16[3584,128]{1,0:T(8,128)(2,1)S(1)} all-gather(bf16[56,128]{1,0:T(8,128)(2,1)S(1)} %copy-done.4), channel_id=1, replica_groups=mesh['dp'=64,'mp'=4] {'dp'}, dimensions={0}, use_global_device_ids=true | all-gather | bytes 931840 | tf_op jit(solution)/shard_map/all_gather | solution.py:64
  202.2 1.2 fusion.23
  203.8 180.0 %all_gather.12 = bf16[3584,128]{1,0:T(8,128)(2,1)S(1)} all-gather(bf16[56,128]{1,0:T(8,128)(2,1)S(1)} %copy-done.5), channel_id=1, replica_groups=mesh['dp'=64,'mp'=4] {'dp'}, dimensions={0}, use_global_device_ids=true | all-gather | bytes 931840 | tf_op jit(solution)/shard_map/all_gather | solution.py:65
  383.8 1.2 convolution_convert_fusion.1
  385.0 9.2 fusion.22
  394.2 1.6 reshape.123
  395.8 0.8 slice_negate_fusion
  396.5 0.6 maximum_multiply_fusion
  397.4 1.3 copy-done.3
  398.7 1.0 fusion
  399.7 1.0 reshape.124
  400.7 2.0 fusion.25
  402.8 0.5 fusion.1
  403.2 0.3 copy.31
  403.6 8.9 fusion.4
  412.8 6.0 convert_element_type.43
  419.1 0.4 compare_reduce_fusion
  419.7 0.6 fusion.24
  420.3 60.5 %reduce-scatter.2.cloned.1.call-done = f32[128,3584]{1,0:T(8,128)} async-done(((f32[512,3584]{1,0:T(8,128)}), f32[128,3584]{1,0:T(8,128)}) %reduce-scatter.2.cloned.1.call-update) | async-done | bytes 1835024 | tf_op jit(solution)/shard_map/reduce_scatter | solution.py:96
  480.9 2.5 multiply_reduce_fusion.1
  483.4 1.8 scatter_custom_fusion
  485.3 1.3 fusion.14
  486.6 1.8 convolution_multiply_fusion.1
  488.5 59.8 %all-reduce.5.cloned.1.call-done = f32[128,3584]{1,0:T(8,128)} async-done(((f32[128,3584]{1,0:T(8,128)}), f32[128,3584]{1,0:T(8,128)}) %all-reduce.5.cloned.1.call-update) | async-done | bytes 1835024 | tf_op jit(solution)/shard_map/psum | solution.py:135
  548.3 7.8 all-reduce.1
  556.2 184.4 %all-reduce = (f32[]{:T(128)}, f32[]{:T(128)}) all-reduce(f32[]{:T(128)} %get-tuple-element.5, f32[]{:T(128)} %get-tuple-element.6), channel_id=1, replica_groups=mesh['dp'=64,'mp'=4] {'dp'}, use_global_device_ids=true, to_apply=%region_9.10 | all-reduce | flops 2 | bytes 16 | tf_op jit(solution)/shard_map/psum | solution.py:134
  741.9 2.6 convolution_multiply_fusion
  744.4 496.6 %all-reduce.7.cloned.1.call-done = f32[128,3584]{1,0:T(8,128)} async-done(((f32[128,3584]{1,0:T(8,128)}), f32[128,3584]{1,0:T(8,128)}) %all-reduce.7.cloned.1.call-update) | async-done | bytes 1835024 | tf_op jit(solution)/shard_map/psum | solution.py:134
  1241.0 2.9 broadcast_multiply_fusion
  (49 shorter events, 1.9 us)
Async XLA Ops:
  7.2 478.1 %copy-start = (bf16[128,3584]{1,0:T(8,128)(2,1)S(1)}, bf16[128,3584]{1,0:T(8,128)(2,1)}, u32[]{:S(2)}) copy-start(bf16[128,3584]{1,0:T(8,128)(2,1)} %param.22) | copy-start | bytes 2752516
  7.2 1.5 copy-start.6
  7.2 377.8 %all-gather.3.cloned.1.call-start = ((), (), s32[]{:S(2)}) async-start(), calls=%async_computation.1 | async-start | bytes 6522880 | tf_op jit(solution)/shard_map/all_gather | solution.py:63
  7.2 4.8 copy-start.4
  7.9 395.6 %all-gather.5.cloned.1.call-start = ((), (), s32[]{:S(2)}) async-start(), calls=%async_computation.2 | async-start | bytes 6522880 | tf_op jit(solution)/shard_map/all_gather | solution.py:92
  8.7 472.2 %reduce-scatter.2.cloned.1.call-start = ((), (), s32[]{:S(2)}) async-start(), calls=%async_computation.3 | async-start | bytes 9175040 | tf_op jit(solution)/shard_map/reduce_scatter | solution.py:96
  9.0 193.2 %copy-start.1 = (bf16[512,3584]{1,0:T(8,128)(2,1)S(1)}, bf16[512,3584]{1,0:T(8,128)(2,1)}, u32[]{:S(2)}) copy-start(bf16[512,3584]{1,0:T(8,128)(2,1)} %param.12) | copy-start | bytes 11010052
  9.0 193.2 %copy-start.9 = (f32[3584]{0:T(1024)S(1)}, f32[3584]{0:T(1024)}, u32[]{:S(2)}) copy-start(f32[3584]{0:T(1024)} %param.14) | copy-start | bytes 43012
  202.2 1.6 copy-start.5
  397.2 1.5 copy-start.3
  412.5 135.8 %all-reduce.5.cloned.1.call-start = ((), (), s32[]{:S(2)}) async-start(), calls=%async_computation.4 | async-start | bytes 3670016 | tf_op jit(solution)/shard_map/psum | solution.py:135
  412.7 6.2 copy-start.7
  412.8 6.9 copy-start.10
  412.8 6.9 copy-start.8
  418.8 64.6 %copy-start.2 = (bf16[256,3584]{1,0:T(8,128)(2,1)S(1)}, bf16[256,3584]{1,0:T(8,128)(2,1)}, u32[]{:S(2)}) copy-start(bf16[256,3584]{1,0:T(8,128)(2,1)} %param.19) | copy-start | bytes 5505028
  488.4 752.6 %all-reduce.7.cloned.1.call-start = ((), (), s32[]{:S(2)}) async-start(), calls=%async_computation.5 | async-start | bytes 3670016 | tf_op jit(solution)/shard_map/psum | solution.py:134
Sparse Core Ops, SparseCore 0:
  11.7 146.0 all-gather.2
  161.5 139.9 all-gather.4
  412.6 68.2 reduce-scatter.1
  488.6 59.6 all-reduce.4
  550.8 690.1 all-reduce.6
